TPU v7x, 32 devices: a whole 2x2x4 slice. The times are simulated.
32 devices in a mesh: dp: 8 (over y, x, core), head: 4 (over z).
Axes of the slice: x: 2, y: 2, z: 4, core: 2. Of those that a mesh axis runs over, the one named last changes fastest.
Arguments:
- tokens: bfloat16 [2048, 2048], P('dp'), may hold values from -6 to 6
- weights: bfloat16 [4, 768, 2048], P('head', 'dp'), may hold values from -0.13479223 to 0.13479223, as said below
- query_gain: float32 [128], replicated, may hold values from 0.25 to 1.75
- key_gain: float32 [128], replicated, may hold values from 0.25 to 1.75
- first_row: int32 [2048], P('dp'), may hold values from 0 to 2047, as said below
- cotangent: bfloat16 [2048, 2048], P('dp', 'head'), may hold values from -6 to 6
Outputs:
- attended: bfloat16 [2048, 2048], P('dp', 'head')
- token_grad: bfloat16 [2048, 2048], P('dp', 'head')
- weight_grad: float32 [4, 768, 2048], P('head', 'dp')
Inputs may be any that keep to these rules, and one draw needn't show every extreme that they name: first_row[i] is the position of the first row of row i's document: documents are runs of consecutive rows, each at most 512 rows long, one of exactly 512 rows, and the last row begins a document of its own. For every even g, weights[g] and weights[g + 1] are equal in their last 256 rows: each key-value head is held by two head devices.
All inputs are finite; a program needn't handle non-finite values.
Results may differ from a plain program's by a relative error of at most 0.017.
Values may be sent and summed in bfloat16 or wider, within the bound.
No kernel may reach another device: no remote copies, remote signals or barrier semaphores. Data moves between devices by JAX's collectives and lax.ppermute only.
A program may use at most 64 MiB of HBM per device.

v0:
```python
import math
import jax
import jax.numpy as jnp
from jax import lax
from jax.sharding import PartitionSpec as P

HD = 128
QH_DEV = 4
COLS = 768
ROWS = 256
SPAN = 2
EPSILON = 1e-06
THETA = 1000000.0
STRETCH = 0.25


def from_behind(x, axis, by):
    devices = lax.axis_size(axis)
    pairs = [(i, i + by) for i in range(devices) if 0 <= i + by < devices]
    return lax.ppermute(x, axis, pairs)


def partner(x, axis, apart):
    return lax.ppermute(x, axis, [(i, i ^ 1 << apart) for i in range(lax.axis_size(axis))])


def rope_tables(position, head_size):
    middle = head_size // 2
    channel = jnp.arange(middle, dtype=jnp.float32)
    frequency = THETA ** (-2.0 * channel / head_size)
    angles = (position.astype(jnp.float32) * STRETCH)[:, None] * frequency[None, :]
    angles = jnp.concatenate([angles, angles], axis=1)
    return (jnp.cos(angles), jnp.sin(angles))


def normalize_rotate(values, scaling, cosine_table, sine_table):
    factor = lax.rsqrt(jnp.mean(values * values, axis=-1, keepdims=True) + EPSILON)
    normed = values * factor * scaling
    middle = normed.shape[-1] // 2
    turned = jnp.concatenate([-normed[..., middle:], normed[..., :middle]], axis=-1)
    return normed * cosine_table + turned * sine_table


def prepare(projected, query_gain, key_gain, cosine_table, sine_table):
    row_count = projected.shape[0]
    queries = projected[:, : QH_DEV * HD].reshape(row_count, QH_DEV, HD)
    queries = normalize_rotate(
        queries, query_gain, cosine_table[:, None, :], sine_table[:, None, :]
    )
    key_part = normalize_rotate(
        projected[:, QH_DEV * HD : (QH_DEV + 1) * HD], key_gain, cosine_table, sine_table
    )
    value_part = projected[:, (QH_DEV + 1) * HD :]
    return (queries, key_part, value_part)


def attend_window(queries, window, upstream, first_rows, query_place, key_place):
    score_scale = 1.0 / math.sqrt(HD)
    key_window = window[:, :HD]
    value_window = window[:, HD:]
    visible = (key_place[None, :] >= first_rows[:, None]) & (
        key_place[None, :] <= query_place[:, None]
    )
    score = (
        jnp.einsum("rhc,kc->rhk", queries, key_window, preferred_element_type=jnp.float32)
        * score_scale
    )
    weight = jnp.where(visible[:, None, :], jnp.exp(score), 0.0)
    denominator = jnp.sum(weight, axis=-1)
    summed = jnp.einsum(
        "rhk,kc->rhc", weight.astype(jnp.bfloat16), value_window, preferred_element_type=jnp.float32
    )
    attended = (summed / denominator[..., None]).astype(jnp.bfloat16)
    probability = weight / denominator[..., None]
    row_delta = jnp.sum(upstream.astype(jnp.float32) * attended.astype(jnp.float32), axis=-1)
    grad_prob = jnp.einsum(
        "rhc,kc->rhk", upstream, value_window, preferred_element_type=jnp.float32
    )
    grad_score = (probability * (grad_prob - row_delta[..., None]) * score_scale).astype(
        jnp.bfloat16
    )
    grad_query = jnp.einsum(
        "rhk,kc->rhc", grad_score, key_window, preferred_element_type=jnp.float32
    )
    grad_key = jnp.einsum("rhk,rhc->kc", grad_score, queries, preferred_element_type=jnp.float32)
    grad_value = jnp.einsum(
        "rhk,rhc->kc",
        probability.astype(jnp.bfloat16),
        upstream,
        preferred_element_type=jnp.float32,
    )
    return (attended, grad_query, jnp.concatenate([grad_key, grad_value], axis=1))


def body(tokens, weights, query_gain, key_gain, first_row, cotangent):
    block_index = lax.axis_index("dp")
    position = block_index * ROWS + jnp.arange(ROWS, dtype=jnp.int32)
    key_place = (block_index - SPAN) * ROWS + jnp.arange((SPAN + 1) * ROWS, dtype=jnp.int32)
    cosine_table, sine_table = rope_tables(position, HD)
    weight_piece = lax.all_gather(weights, "dp", axis=1, tiled=True)
    projected = jnp.einsum("rd,cd->rc", tokens, weight_piece[0], preferred_element_type=jnp.float32)
    prepared, pullback = jax.vjp(
        lambda values: prepare(values, query_gain, key_gain, cosine_table, sine_table), projected
    )
    queries = prepared[0].astype(jnp.bfloat16)
    key_value = jnp.concatenate([prepared[1], prepared[2]], axis=1).astype(jnp.bfloat16)
    earlier = [from_behind(key_value, "dp", distance) for distance in range(SPAN, 0, -1)]
    window = jnp.concatenate(earlier + [key_value], axis=0)
    upstream = cotangent.reshape(ROWS, QH_DEV, HD)
    attended, grad_query, slot_grads = attend_window(
        queries, window, upstream, first_row, position, key_place
    )
    pair_grad = slot_grads[SPAN * ROWS :]
    for distance in range(1, SPAN + 1):
        slot_index = SPAN - distance
        pair_grad = pair_grad + from_behind(
            slot_grads[slot_index * ROWS : (slot_index + 1) * ROWS].astype(jnp.bfloat16),
            "dp",
            -distance,
        ).astype(jnp.float32)
    grad_projected = pullback((grad_query, pair_grad[:, :HD], pair_grad[:, HD:]))[0].astype(
        jnp.bfloat16
    )
    partial_grad = jnp.dot(grad_projected, weight_piece[0], preferred_element_type=jnp.float32)
    token_grad = lax.psum_scatter(
        partial_grad.astype(jnp.bfloat16), "head", scatter_dimension=1, tiled=True
    )
    shard_rows = COLS // lax.axis_size("dp")
    own_grad = lax.psum_scatter(
        jnp.einsum("rc,rd->cd", grad_projected, tokens, preferred_element_type=jnp.float32),
        "dp",
        scatter_dimension=0,
        tiled=True,
    )
    partner_grad = partner(own_grad.astype(jnp.bfloat16), "head", 0).astype(own_grad.dtype)
    global_rows = block_index * shard_rows + jnp.arange(shard_rows, dtype=jnp.int32)
    shared_rows = global_rows >= QH_DEV * HD
    weight_grad = jnp.where(shared_rows[:, None], own_grad + partner_grad, own_grad)
    return (attended.reshape(ROWS, QH_DEV * HD), token_grad, weight_grad[None])


def solution(mesh):
    in_specs = (P("dp", None), P("head", "dp", None), P(), P(), P("dp"), P("dp", "head"))
    out_specs = (P("dp", "head"), P("dp", "head"), P("head", "dp", None))
    return jax.shard_map(body, mesh=mesh, in_specs=in_specs, out_specs=out_specs, check_vma=False)
```

profile of v0, /device:TPU:0, one launch (start us, length us, event | category | flops | bytes accessed | tf_op | source)
XLA Modules:
  0.0 185.5 jit_solution(12164193166599489742)
XLA Ops:
  8.0 1.8 copy.66
  9.9 1.6 compare_and_fusion
  11.5 33.3 %all-gather.2.cloned.1.call-done = bf16[1,768,2048]{2,1,0:T(8,128)(2,1)} async-done(((bf16[1,96,2048]{2,1,0:T(8,128)(2,1)}), bf16[1,768,2048]{2,1,0:T(8,128)(2,1)}) %all-gather.2.cloned.1.call-update) | async-done | bytes 3145744 | tf_op jit(solution)/shard_map/all_gather | solution.py:100
  44.8 2.9 %fusion.4 = f32[256,768]{1,0:T(8,128)S(1)} fusion(bf16[256,2048]{1,0:T(8,128)(2,1)S(1)} %copy-done, bf16[1,768,2048]{2,1,0:T(8,128)(2,1)} %all-gather.2.cloned.1.call-done), kind=kOutput, calls=%fused_computation.5 | convolution fusion | flops 805306368 | bytes 4980736 | tf_op jit(solution)/shard_map/rd,cd->rc/dot_general | solution.py:101
  48.1 1.3 fusion.39
  50.0 2.8 %collective-permute-start.1 = (bf16[256,256]{1,0:T(8,128)(2,1)}, bf16[256,256]{1,0:T(8,128)(2,1)}, u32[]{:S(2)}, u32[]{:S(2)}) collective-permute-start(bf16[256,256]{1,0:T(8,128)(2,1)} %pad_maximum_fusion.2), channel_id=1, source_target_pairs={{0,4},{4,8},{8,12},{12,16},{16,20},{20,24},{24,28},{1,5},{5,9},{9,... | collective-permute-start | bytes 393224 | tf_op jit(solution)/shard_map/ppermute | solution.py:20
  52.8 3.4 %collective-permute-start = (bf16[256,256]{1,0:T(8,128)(2,1)}, bf16[256,256]{1,0:T(8,128)(2,1)}, u32[]{:S(2)}, u32[]{:S(2)}) collective-permute-start(bf16[256,256]{1,0:T(8,128)(2,1)} %pad_maximum_fusion.2), channel_id=1, source_target_pairs={{0,8},{4,12},{8,16},{12,20},{16,24},{20,28},{1,9},{5,13},{9,17},{1... | collective-permute-start | bytes 393224 | tf_op jit(solution)/shard_map/ppermute | solution.py:20
  57.0 1.0 copy.63
  60.5 1.0 fusion.10
  61.6 1.4 multiply_reduce_fusion.1
  63.0 1.1 fusion.19
  64.1 1.5 fusion.1
  67.8 1.3 collective-permute-start.2
  69.1 1.3 collective-permute-start.3
  71.4 7.2 %collective-permute-done.3 = bf16[256,256]{1,0:T(8,128)(2,1)} collective-permute-done((bf16[256,256]{1,0:T(8,128)(2,1)}, bf16[256,256]{1,0:T(8,128)(2,1)}, u32[]{:S(2)}, u32[]{:S(2)}) %collective-permute-start.3) | collective-permute-done | bytes 131104 | tf_op jit(solution)/shard_map/ppermute | solution.py:20
  78.6 1.1 fusion.35
  81.1 3.7 %fusion.48 = f32[768,2048]{1,0:T(8,128)} fusion(bf16[256,2048]{1,0:T(8,128)(2,1)S(1)} %copy-done, f32[256,512]{1,0:T(8,128)S(1)} %copy.87, f32[256,128]{1,0:T(8,128)S(1)} %add_add_fusion.1, f32[256,128]{1,0:T(8,128)S(1)} %get-tuple-element.23), kind=kOutput, calls=%fused_computation.82 | convolution fusion | flops 805896192 | bytes 8126464 | tf_op jit(solution)/shard_map/rc,rd->cd/dot_general | solution.py:130
  84.9 3.9 %fusion.6 = bf16[256,2048]{1,0:T(8,128)(2,1)} fusion(bf16[1,768,2048]{2,1,0:T(8,128)(2,1)} %all-gather.2.cloned.1.call-done, f32[256,512]{1,0:T(8,128)S(1)} %copy.87, f32[256,128]{1,0:T(8,128)S(1)} %add_add_fusion.1, f32[256,128]{1,0:T(8,128)S(1)} %get-tuple-element.23), kind=kOutput, calls=%fused_computation.8 | convolution fusion | flops 806420480 | bytes 4980736 | tf_op jit(solution)/shard_map/dot_general | solution.py:124
  88.8 59.1 %reduce-scatter.5.cloned.1.call-done = f32[96,2048]{1,0:T(8,128)} async-done(((f32[768,2048]{1,0:T(8,128)}), f32[96,2048]{1,0:T(8,128)}) %reduce-scatter.5.cloned.1.call-update) | async-done | bytes 786448 | tf_op jit(solution)/shard_map/reduce_scatter | solution.py:129
  147.9 1.2 convert_element_type.61
  149.1 1.6 collective-permute-start.4
  151.5 11.0 %collective-permute-done.4 = bf16[96,2048]{1,0:T(8,128)(2,1)S(1)} collective-permute-done((bf16[96,2048]{1,0:T(8,128)(2,1)S(1)}, bf16[96,2048]{1,0:T(8,128)(2,1)S(1)}, u32[]{:S(2)}, u32[]{:S(2)}) %collective-permute-start.4) | collective-permute-done | bytes 393248 | tf_op jit(solution)/shard_map/ppermute | solution.py:24
  162.5 2.2 %fusion.29 = f32[1,96,2048]{2,1,0:T(8,128)} fusion(f32[96,2048]{1,0:T(8,128)} %reduce-scatter.5.cloned.1.call-done, bf16[96,2048]{1,0:T(8,128)(2,1)S(1)} %collective-permute-done.4, pred[96]{0:T(512)(128)(4,1)S(1)} %add_compare_fusion), kind=kLoop, calls=%fused_computation.27 | loop fusion | flops 589824 | bytes 1966176 | tf_op jit(solution)/shard_map/broadcast_in_dim | solution.py:139
  164.7 14.3 %reduce-scatter.3.cloned.1.call-done = bf16[256,512]{1,0:T(8,128)(2,1)} async-done(((bf16[256,2048]{1,0:T(8,128)(2,1)}), bf16[256,512]{1,0:T(8,128)(2,1)}) %reduce-scatter.3.cloned.1.call-update) | async-done | bytes 262160 | tf_op jit(solution)/shard_map/reduce_scatter | solution.py:125
  (61 shorter events, 10.6 us)
Async XLA Ops:
  7.2 37.7 %copy-start = (bf16[256,2048]{1,0:T(8,128)(2,1)S(1)}, bf16[256,2048]{1,0:T(8,128)(2,1)}, u32[]{:S(2)}) copy-start(bf16[256,2048]{1,0:T(8,128)(2,1)} %param.6) | copy-start | bytes 3145732
  7.2 37.6 %all-gather.2.cloned.1.call-start = ((), (), s32[]{:S(2)}) async-start(), calls=%async_computation.2 | async-start | bytes 3538944 | tf_op jit(solution)/shard_map/all_gather | solution.py:100
  7.9 140.0 %reduce-scatter.5.cloned.1.call-start = ((), (), s32[]{:S(2)}) async-start(), calls=%async_computation.4 | async-start | bytes 7077888 | tf_op jit(solution)/shard_map/reduce_scatter | solution.py:129
  9.8 38.1 %copy-start.6 = (f32[128]{0:T(128)S(1)}, f32[128]{0:T(128)}, u32[]{:S(2)}) copy-start(f32[128]{0:T(128)} %param.9) | copy-start | bytes 1540
  47.9 10.4 %copy-start.5 = (f32[128]{0:T(128)S(1)}, f32[128]{0:T(128)}, u32[]{:S(2)}) copy-start(f32[128]{0:T(128)} %param.8) | copy-start | bytes 1540
  50.0 8.5 %collective-permute-start.1 = (bf16[256,256]{1,0:T(8,128)(2,1)}, bf16[256,256]{1,0:T(8,128)(2,1)}, u32[]{:S(2)}, u32[]{:S(2)}) collective-permute-start(bf16[256,256]{1,0:T(8,128)(2,1)} %pad_maximum_fusion.2), channel_id=1, source_target_pairs={{0,4},{4,8},{8,12},{12,16},{16,20},{20,24},{24,28},{1,5},{5,9},{9,... | collective-permute-start | bytes 393224 | tf_op jit(solution)/shard_map/ppermute | solution.py:20
  52.8 6.7 %collective-permute-start = (bf16[256,256]{1,0:T(8,128)(2,1)}, bf16[256,256]{1,0:T(8,128)(2,1)}, u32[]{:S(2)}, u32[]{:S(2)}) collective-permute-start(bf16[256,256]{1,0:T(8,128)(2,1)} %pad_maximum_fusion.2), channel_id=1, source_target_pairs={{0,8},{4,12},{8,16},{12,20},{16,24},{20,28},{1,9},{5,13},{9,17},{1... | collective-permute-start | bytes 393224 | tf_op jit(solution)/shard_map/ppermute | solution.py:20
  58.2 2.3 %copy-start.4 = (pred[256,768]{1,0:T(8,128)(4,1)S(1)}, pred[256,768]{1,0:T(8,128)(4,1)}, u32[]{:S(2)}) copy-start(pred[256,768]{1,0:T(8,128)(4,1)} %compare_and_fusion) | copy-start | bytes 589828
  58.4 3.1 %copy-start.3 = (bf16[256,512]{0,1:T(8,128)(2,1)S(1)}, bf16[256,512]{0,1:T(8,128)(2,1)}, u32[]{:S(2)}) copy-start(bf16[256,512]{0,1:T(8,128)(2,1)} %copy.66) | copy-start | bytes 786436
  64.1 3.0 %copy-start.1 = (f32[768,128]{1,0:T(8,128)}, f32[768,128]{1,0:T(8,128)S(1)}, u32[]{:S(2)}) copy-start(f32[768,128]{1,0:T(8,128)S(1)} %fusion.19) | copy-start | bytes 1179652
  67.8 3.6 %collective-permute-start.2 = (bf16[256,256]{1,0:T(8,128)(2,1)}, bf16[256,256]{1,0:T(8,128)(2,1)}, u32[]{:S(2)}, u32[]{:S(2)}) collective-permute-start(bf16[256,256]{1,0:T(8,128)(2,1)} %get-tuple-element.21), channel_id=1, source_target_pairs={{4,0},{8,4},{12,8},{16,12},{20,16},{24,20},{28,24},{5,1},{9,5},{13... | collective-permute-start | bytes 393224 | tf_op jit(solution)/shard_map/ppermute | solution.py:20
  69.1 9.5 %collective-permute-start.3 = (bf16[256,256]{1,0:T(8,128)(2,1)}, bf16[256,256]{1,0:T(8,128)(2,1)}, u32[]{:S(2)}, u32[]{:S(2)}) collective-permute-start(bf16[256,256]{1,0:T(8,128)(2,1)} %get-tuple-element.22), channel_id=1, source_target_pairs={{8,0},{12,4},{16,8},{20,12},{24,16},{28,20},{9,1},{13,5},{17,9},{2... | collective-permute-start | bytes 393224 | tf_op jit(solution)/shard_map/ppermute | solution.py:20
  84.8 65.8 %copy-start.2 = (bf16[256,4,128]{0,2,1:T(8,128)(2,1)S(1)}, bf16[256,4,128]{0,2,1:T(8,128)(2,1)}, u32[]{:S(2)}) copy-start(bf16[256,4,128]{0,2,1:T(8,128)(2,1)} %get-tuple-element.35) | copy-start | bytes 786436
  84.8 94.1 %reduce-scatter.3.cloned.1.call-start = ((), (), s32[]{:S(2)}) async-start(), calls=%async_computation.3 | async-start | bytes 1310720 | tf_op jit(solution)/shard_map/reduce_scatter | solution.py:125
  149.1 13.5 %collective-permute-start.4 = (bf16[96,2048]{1,0:T(8,128)(2,1)S(1)}, bf16[96,2048]{1,0:T(8,128)(2,1)S(1)}, u32[]{:S(2)}, u32[]{:S(2)}) collective-permute-start(bf16[96,2048]{1,0:T(8,128)(2,1)S(1)} %convert_element_type.61), channel_id=1, source_target_pairs={{0,1},{1,0},{2,3},{3,2},{4,5},{5,4},{6,7},{7,6},{8,9},{9,8},{10,11... | collective-permute-start | bytes 1179656 | tf_op jit(solution)/shard_map/ppermute | solution.py:24
Sparse Core Ops, SparseCore 0:
  9.9 34.8 all-gather.1
  84.9 62.8 reduce-scatter.4
  150.8 28.1 reduce-scatter.2
where the time goes:
time: 186 us
  waiting for transfers between devices  127 us (68%)
  matrix products  16.7 us (9%)
  between operations  14.1 us (8%)
  other arithmetic  11.9 us (6%)
  starting transfers between devices  10.4 us (6%)
  local copies, waits for them, and re-layouts  5.22 us (3%)
    reduce_scatter x1, waiting for transfers between devices, body(): lax.psum_scatter(jnp.einsum('rc,rd->cd', grad_projected, tokens, preferre...  59.1 us
    all_gather x1, waiting for transfers between devices, body(): weight_piece = lax.all_gather(weights, 'dp', axis=1, tiled=True)  33.3 us
    reduce_scatter x1, waiting for transfers between devices, body(): lax.psum_scatter(partial_grad.astype(jnp.bfloat16), 'head', scatter_dimen...  14.3 us
    ppermute x1, waiting for transfers between devices, partner(): lax.ppermute(x, axis, [(i, i ^ 1 << apart) for i in range(lax.axis_size(a...  11 us
    ppermute x4, starting transfers between devices, from_behind(): return lax.ppermute(x, axis, pairs)  8.74 us
    ppermute x4, waiting for transfers between devices, from_behind(): return lax.ppermute(x, axis, pairs)  8.71 us
    dot_general x1, matrix products, body(): jnp.dot(grad_projected, weight_piece[0], preferred_element_type=jnp.float32)  3.86 us
  transfers between devices with their start and end apart: 8, of which 7 were waited for; matrix products, arithmetic and copies ran while one was open for 8% of the time, Pallas kernels for 0%

commit v1 on v0

--- a/solution.py
+++ b/solution.py
@@ -12,6 +12,19 @@
 EPSILON = 1e-06
 THETA = 1000000.0
 STRETCH = 0.25
+
+
+def gather_around(x, axis, dim):
+    ways = lax.axis_size(axis)
+    up = [(d, (d + 1) % ways) for d in range(ways)]
+    down = [(d, (d - 1) % ways) for d in range(ways)]
+    earlier, later = ([x], [x])
+    for _ in range(ways // 2):
+        earlier.append(lax.ppermute(earlier[-1], axis, up))
+    for _ in range((ways - 1) // 2):
+        later.append(lax.ppermute(later[-1], axis, down))
+    line = jnp.concatenate([*earlier[::-1], *later[1:]], axis=dim)
+    return jnp.roll(line, (lax.axis_index(axis) - ways // 2) * x.shape[dim], axis=dim)
 
 
 def from_behind(x, axis, by):
@@ -97,7 +110,7 @@
     position = block_index * ROWS + jnp.arange(ROWS, dtype=jnp.int32)
     key_place = (block_index - SPAN) * ROWS + jnp.arange((SPAN + 1) * ROWS, dtype=jnp.int32)
     cosine_table, sine_table = rope_tables(position, HD)
-    weight_piece = lax.all_gather(weights, "dp", axis=1, tiled=True)
+    weight_piece = gather_around(weights, "dp", 1)
     projected = jnp.einsum("rd,cd->rc", tokens, weight_piece[0], preferred_element_type=jnp.float32)
     prepared, pullback = jax.vjp(
         lambda values: prepare(values, query_gain, key_gain, cosine_table, sine_table), projected

time: 186 us -> 192 us (1.032)
  starting transfers between devices: 10.4 us -> 19.5 us
  other arithmetic: 11.9 us -> 7.24 us
  local copies, waits for them, and re-layouts: 5.22 us -> 8.85 us
  matrix products: 16.7 us -> 13.9 us
    all_gather x1 -> x0, waiting for transfers between devices: 33.3 us -> none  [body(): weight_piece = lax.all_gather(weights, 'dp', axis=1, tiled=True)]
    ppermute x0 -> x7, waiting for transfers between devices: none -> 31.3 us  [the longest x4 31.3 us: gather_around(): earlier.append(lax.ppermute(earlier[-1], axis, up))]
    ppermute x0 -> x7, starting transfers between devices: none -> 8.58 us  [the longest x3 8.03 us: gather_around(): later.append(lax.ppermute(later[-1], axis, down))]
    unnamed x16 -> x27, local copies, waits for them, and re-layouts: 2.68 us -> 8.79 us
  transfers between devices with their start and end apart: 8 -> 14, of which waited for: 7 -> 9; matrix products, arithmetic and copies ran while one was open for 8% -> 7% of each run, Pallas kernels for 0% -> 0%
where the time goes in v1:
time: 192 us; the launch traced here: 191 us
  waiting for transfers between devices  127 us (66%)
  starting transfers between devices  19.5 us (10%)
  between operations  14.5 us (8%)
  matrix products  13.9 us (7%)
  local copies, waits for them, and re-layouts  8.85 us (5%)
  other arithmetic  7.24 us (4%)
    reduce_scatter x1, waiting for transfers between devices, body(): lax.psum_scatter(jnp.einsum('rc,rd->cd', grad_projected, tokens, preferre...  60.8 us
    ppermute x4, waiting for transfers between devices, gather_around(): earlier.append(lax.ppermute(earlier[-1], axis, up))  31.3 us
    reduce_scatter x1, waiting for transfers between devices, body(): lax.psum_scatter(partial_grad.astype(jnp.bfloat16), 'head', scatter_dimen...  14.2 us
    ppermute x1, waiting for transfers between devices, partner(): lax.ppermute(x, axis, [(i, i ^ 1 << apart) for i in range(lax.axis_size(a...  11.1 us
    ppermute x4, waiting for transfers between devices, from_behind(): return lax.ppermute(x, axis, pairs)  9.55 us
    ppermute x4, starting transfers between devices, from_behind(): return lax.ppermute(x, axis, pairs)  9.33 us
    unnamed x27, local copies, waits for them, and re-layouts  8.79 us
    ppermute x3, starting transfers between devices, gather_around(): later.append(lax.ppermute(later[-1], axis, down))  8.03 us
  transfers between devices with their start and end apart: 14, of which 9 were waited for; matrix products, arithmetic and copies ran while one was open for 7% of the time, Pallas kernels for 0%

profile of v1, /device:TPU:0, one launch (start us, length us, event | category | flops | bytes accessed | tf_op | source)
XLA Modules:
  0.0 191.1 jit_solution(8535409103176682693)
XLA Ops:
  7.8 8.5 %collective-permute-done = bf16[1,96,2048]{2,1,0:T(8,128)(2,1)S(1)} collective-permute-done((bf16[1,96,2048]{2,1,0:T(8,128)(2,1)}, bf16[1,96,2048]{2,1,0:T(8,128)(2,1)S(1)}, u32[]{:S(2)}, u32[]{:S(2)}) %collective-permute-start) | collective-permute-done | bytes 393248 | tf_op jit(solution)/shard_map/ppermute | solution.py:23
  16.3 2.6 %collective-permute-start.4 = (bf16[1,96,2048]{2,1,0:T(8,128)(2,1)}, bf16[1,96,2048]{2,1,0:T(8,128)(2,1)S(1)}, u32[]{:S(2)}, u32[]{:S(2)}) collective-permute-start(bf16[1,96,2048]{2,1,0:T(8,128)(2,1)} %param.7), channel_id=1, source_target_pairs={{0,28},{4,0},{8,4},{12,8},{16,12},{20,16},{24,20},{28,24},{1,29},{... | collective-permute-start | bytes 1179656 | tf_op jit(solution)/shard_map/ppermute | solution.py:25
  19.0 7.8 %collective-permute-done.1 = bf16[1,96,2048]{2,1,0:T(8,128)(2,1)S(1)} collective-permute-done((bf16[1,96,2048]{2,1,0:T(8,128)(2,1)S(1)}, bf16[1,96,2048]{2,1,0:T(8,128)(2,1)S(1)}, u32[]{:S(2)}, u32[]{:S(2)}) %collective-permute-start.1) | collective-permute-done | bytes 393248 | tf_op jit(solution)/shard_map/ppermute | solution.py:23
  26.8 2.7 %collective-permute-start.5 = (bf16[1,96,2048]{2,1,0:T(8,128)(2,1)S(1)}, bf16[1,96,2048]{2,1,0:T(8,128)(2,1)}, u32[]{:S(2)}, u32[]{:S(2)}) collective-permute-start(bf16[1,96,2048]{2,1,0:T(8,128)(2,1)S(1)} %collective-permute-done.4), channel_id=1, source_target_pairs={{0,28},{4,0},{8,4},{12,8},{16,12},{20,16},{24,20},{28,24},{1,29},{... | collective-permute-start | bytes 1179656 | tf_op jit(solution)/shard_map/ppermute | solution.py:25
  29.5 8.2 %collective-permute-done.2 = bf16[1,96,2048]{2,1,0:T(8,128)(2,1)S(1)} collective-permute-done((bf16[1,96,2048]{2,1,0:T(8,128)(2,1)S(1)}, bf16[1,96,2048]{2,1,0:T(8,128)(2,1)S(1)}, u32[]{:S(2)}, u32[]{:S(2)}) %collective-permute-start.2) | collective-permute-done | bytes 393248 | tf_op jit(solution)/shard_map/ppermute | solution.py:23
  37.7 1.1 copy.11
  39.8 2.7 %collective-permute-start.6 = (bf16[1,96,2048]{2,1,0:T(8,128)(2,1)}, bf16[1,96,2048]{2,1,0:T(8,128)(2,1)S(1)}, u32[]{:S(2)}, u32[]{:S(2)}) collective-permute-start(bf16[1,96,2048]{2,1,0:T(8,128)(2,1)} %collective-permute-done.5), channel_id=1, source_target_pairs={{0,28},{4,0},{8,4},{12,8},{16,12},{20,16},{24,20},{28,24},{1,29},{... | collective-permute-start | bytes 1179656 | tf_op jit(solution)/shard_map/ppermute | solution.py:25
  42.5 6.8 %collective-permute-done.3 = bf16[1,96,2048]{2,1,0:T(8,128)(2,1)} collective-permute-done((bf16[1,96,2048]{2,1,0:T(8,128)(2,1)S(1)}, bf16[1,96,2048]{2,1,0:T(8,128)(2,1)}, u32[]{:S(2)}, u32[]{:S(2)}) %collective-permute-start.3) | collective-permute-done | bytes 393248 | tf_op jit(solution)/shard_map/ppermute | solution.py:23
  56.0 1.4 copy-done.2
  58.0 1.5 collective-permute-start.7
  59.5 5.3 %collective-permute-start.8 = (bf16[256,256]{0,1:T(8,128)(2,1)S(1)}, bf16[256,256]{0,1:T(8,128)(2,1)S(1)}, u32[]{:S(2)}, u32[]{:S(2)}) collective-permute-start(bf16[256,256]{0,1:T(8,128)(2,1)S(1)} %pad_maximum_fusion.2), channel_id=1, source_target_pairs={{0,4},{4,8},{8,12},{12,16},{16,20},{20,24},{24,28},{1,5},{5,9},{9,... | collective-permute-start | bytes 393224 | tf_op jit(solution)/shard_map/ppermute | solution.py:33
  65.8 1.0 fusion.12
  68.6 1.4 fusion.1
  71.1 1.3 collective-permute-start.10
  72.4 1.3 collective-permute-start.9
  74.1 9.0 %collective-permute-done.10 = bf16[256,256]{0,1:T(8,128)(2,1)S(1)} collective-permute-done((bf16[256,256]{0,1:T(8,128)(2,1)S(1)}, bf16[256,256]{0,1:T(8,128)(2,1)S(1)}, u32[]{:S(2)}, u32[]{:S(2)}) %collective-permute-start.10) | collective-permute-done | bytes 131104 | tf_op jit(solution)/shard_map/ppermute | solution.py:33
  84.6 3.6 %fusion.55 = f32[768,2048]{1,0:T(8,128)} fusion(bf16[256,2048]{1,0:T(8,128)(2,1)S(1)} %copy-done, f32[256,512]{0,1:T(8,128)S(1)} %bitcast.58, f32[256,128]{0,1:T(8,128)S(1)} %add_add_fusion.1, f32[256,128]{0,1:T(8,128)S(1)} %get-tuple-element.12), kind=kOutput, calls=%fused_computation.103 | convolution fusion | flops 805896192 | bytes 8126464 | tf_op jit(solution)/shard_map/rc,rd->cd/dot_general | solution.py:143
  88.3 4.0 %fusion.8 = bf16[256,2048]{1,0:T(8,128)(2,1)} fusion(bf16[1,1536,2048]{2,1,0:T(8,128)(2,1)} %copy-done.2, s32[]{:T(128)S(6)} %select_n.22, f32[256,512]{0,1:T(8,128)S(1)} %bitcast.59, f32[256,128]{0,1:T(8,128)S(1)} %add_add_fusion.1, f32[256,128]{0,1:T(8,128)S(1)} %get-tuple-element.12), kind=kOutput, calls=%fused_computation.10 | convolution fusion | flops 806420480 | bytes 4980740 | tf_op jit(solution)/shard_map/dot_general | solution.py:137
  92.3 60.8 %reduce-scatter.5.cloned.1.call-done = f32[96,2048]{1,0:T(8,128)} async-done(((f32[768,2048]{1,0:T(8,128)}), f32[96,2048]{1,0:T(8,128)}) %reduce-scatter.5.cloned.1.call-update) | async-done | bytes 786448 | tf_op jit(solution)/shard_map/reduce_scatter | solution.py:142
  153.2 1.2 convert_element_type.61
  154.3 1.5 collective-permute-start.11
  156.7 11.1 %collective-permute-done.11 = bf16[96,2048]{1,0:T(8,128)(2,1)S(1)} collective-permute-done((bf16[96,2048]{1,0:T(8,128)(2,1)S(1)}, bf16[96,2048]{1,0:T(8,128)(2,1)S(1)}, u32[]{:S(2)}, u32[]{:S(2)}) %collective-permute-start.11) | collective-permute-done | bytes 393248 | tf_op jit(solution)/shard_map/ppermute | solution.py:37
  167.8 2.2 %fusion.34 = f32[1,96,2048]{2,1,0:T(8,128)} fusion(f32[96,2048]{1,0:T(8,128)} %reduce-scatter.5.cloned.1.call-done, bf16[96,2048]{1,0:T(8,128)(2,1)S(1)} %collective-permute-done.11, pred[96]{0:T(512)(128)(4,1)S(1)} %add_compare_fusion), kind=kLoop, calls=%fused_computation.30 | loop fusion | flops 589824 | bytes 1966176 | tf_op jit(solution)/shard_map/broadcast_in_dim | solution.py:152
  170.0 14.2 %reduce-scatter.3.cloned.1.call-done = bf16[256,512]{1,0:T(8,128)(2,1)} async-done(((bf16[256,2048]{1,0:T(8,128)(2,1)}), bf16[256,512]{1,0:T(8,128)(2,1)}) %reduce-scatter.3.cloned.1.call-update) | async-done | bytes 262160 | tf_op jit(solution)/shard_map/reduce_scatter | solution.py:138
  (77 shorter events, 15.3 us)
Async XLA Ops:
  7.2 47.7 %copy-start = (bf16[256,2048]{1,0:T(8,128)(2,1)S(1)}, bf16[256,2048]{1,0:T(8,128)(2,1)}, u32[]{:S(2)}) copy-start(bf16[256,2048]{1,0:T(8,128)(2,1)} %param.6) | copy-start | bytes 3145732
  7.2 46.5 %copy-start.1 = (bf16[1,96,2048]{2,1,0:T(8,128)(2,1)S(1)}, bf16[1,96,2048]{2,1,0:T(8,128)(2,1)}, u32[]{:S(2)}) copy-start(bf16[1,96,2048]{2,1,0:T(8,128)(2,1)} %param.7) | copy-start | bytes 1179652
  7.2 146.0 %reduce-scatter.5.cloned.1.call-start = ((), (), s32[]{:S(2)}) async-start(), calls=%async_computation.3 | async-start | bytes 7077888 | tf_op jit(solution)/shard_map/reduce_scatter | solution.py:142
  7.2 9.1 %collective-permute-start = (bf16[1,96,2048]{2,1,0:T(8,128)(2,1)}, bf16[1,96,2048]{2,1,0:T(8,128)(2,1)S(1)}, u32[]{:S(2)}, u32[]{:S(2)}) collective-permute-start(bf16[1,96,2048]{2,1,0:T(8,128)(2,1)} %param.7), channel_id=1, source_target_pairs={{0,4},{4,8},{8,12},{12,16},{16,20},{20,24},{24,28},{28,0},{1,5},{5... | collective-permute-start | bytes 1179656 | tf_op jit(solution)/shard_map/ppermute | solution.py:23
  16.3 10.4 %collective-permute-start.1 = (bf16[1,96,2048]{2,1,0:T(8,128)(2,1)S(1)}, bf16[1,96,2048]{2,1,0:T(8,128)(2,1)S(1)}, u32[]{:S(2)}, u32[]{:S(2)}) collective-permute-start(bf16[1,96,2048]{2,1,0:T(8,128)(2,1)S(1)} %collective-permute-done), channel_id=1, source_target_pairs={{0,4},{4,8},{8,12},{12,16},{16,20},{20,24},{24,28},{28,0},{1,5},{5... | collective-permute-start | bytes 1179656 | tf_op jit(solution)/shard_map/ppermute | solution.py:23
  16.3 10.5 %collective-permute-start.4 = (bf16[1,96,2048]{2,1,0:T(8,128)(2,1)}, bf16[1,96,2048]{2,1,0:T(8,128)(2,1)S(1)}, u32[]{:S(2)}, u32[]{:S(2)}) collective-permute-start(bf16[1,96,2048]{2,1,0:T(8,128)(2,1)} %param.7), channel_id=1, source_target_pairs={{0,28},{4,0},{8,4},{12,8},{16,12},{20,16},{24,20},{28,24},{1,29},{... | collective-permute-start | bytes 1179656 | tf_op jit(solution)/shard_map/ppermute | solution.py:25
  26.7 11.0 %collective-permute-start.2 = (bf16[1,96,2048]{2,1,0:T(8,128)(2,1)S(1)}, bf16[1,96,2048]{2,1,0:T(8,128)(2,1)S(1)}, u32[]{:S(2)}, u32[]{:S(2)}) collective-permute-start(bf16[1,96,2048]{2,1,0:T(8,128)(2,1)S(1)} %collective-permute-done.1), channel_id=1, source_target_pairs={{0,4},{4,8},{8,12},{12,16},{16,20},{20,24},{24,28},{28,0},{1,5},{5... | collective-permute-start | bytes 1179656 | tf_op jit(solution)/shard_map/ppermute | solution.py:23
  26.8 12.9 %collective-permute-start.5 = (bf16[1,96,2048]{2,1,0:T(8,128)(2,1)S(1)}, bf16[1,96,2048]{2,1,0:T(8,128)(2,1)}, u32[]{:S(2)}, u32[]{:S(2)}) collective-permute-start(bf16[1,96,2048]{2,1,0:T(8,128)(2,1)S(1)} %collective-permute-done.4), channel_id=1, source_target_pairs={{0,28},{4,0},{8,4},{12,8},{16,12},{20,16},{24,20},{28,24},{1,29},{... | collective-permute-start | bytes 1179656 | tf_op jit(solution)/shard_map/ppermute | solution.py:25
  37.7 11.5 %collective-permute-start.3 = (bf16[1,96,2048]{2,1,0:T(8,128)(2,1)S(1)}, bf16[1,96,2048]{2,1,0:T(8,128)(2,1)}, u32[]{:S(2)}, u32[]{:S(2)}) collective-permute-start(bf16[1,96,2048]{2,1,0:T(8,128)(2,1)S(1)} %collective-permute-done.2), channel_id=1, source_target_pairs={{0,4},{4,8},{8,12},{12,16},{16,20},{20,24},{24,28},{28,0},{1,5},{5... | collective-permute-start | bytes 1179656 | tf_op jit(solution)/shard_map/ppermute | solution.py:23
  39.8 12.7 %collective-permute-start.6 = (bf16[1,96,2048]{2,1,0:T(8,128)(2,1)}, bf16[1,96,2048]{2,1,0:T(8,128)(2,1)S(1)}, u32[]{:S(2)}, u32[]{:S(2)}) collective-permute-start(bf16[1,96,2048]{2,1,0:T(8,128)(2,1)} %collective-permute-done.5), channel_id=1, source_target_pairs={{0,28},{4,0},{8,4},{12,8},{16,12},{20,16},{24,20},{28,24},{1,29},{... | collective-permute-start | bytes 1179656 | tf_op jit(solution)/shard_map/ppermute | solution.py:25
  53.7 2.3 %copy-start.4 = (f32[128]{0:T(128)S(1)}, f32[128]{0:T(128)}, u32[]{:S(2)}) copy-start(f32[128]{0:T(128)} %param.9) | copy-start | bytes 1540
  54.8 10.1 %copy-start.3 = (f32[128]{0:T(128)S(1)}, f32[128]{0:T(128)}, u32[]{:S(2)}) copy-start(f32[128]{0:T(128)} %param.8) | copy-start | bytes 1540
  54.8 2.7 %copy-start.2 = (bf16[1,1536,2048]{2,1,0:T(8,128)(2,1)}, bf16[1,1536,2048]{2,1,0:T(8,128)(2,1)S(1)}, u32[]{:S(2)}) copy-start(bf16[1,1536,2048]{2,1,0:T(8,128)(2,1)S(1)} %constant_dynamic-update-slice_fusion) | copy-start | bytes 18874372
  58.0 7.2 %collective-permute-start.7 = (bf16[256,256]{0,1:T(8,128)(2,1)S(1)}, bf16[256,256]{0,1:T(8,128)(2,1)S(1)}, u32[]{:S(2)}, u32[]{:S(2)}) collective-permute-start(bf16[256,256]{0,1:T(8,128)(2,1)S(1)} %pad_maximum_fusion.2), channel_id=1, source_target_pairs={{0,8},{4,12},{8,16},{12,20},{16,24},{20,28},{1,9},{5,13},{9,17},{1... | collective-permute-start | bytes 393224 | tf_op jit(solution)/shard_map/ppermute | solution.py:33
  59.5 6.2 %collective-permute-start.8 = (bf16[256,256]{0,1:T(8,128)(2,1)S(1)}, bf16[256,256]{0,1:T(8,128)(2,1)S(1)}, u32[]{:S(2)}, u32[]{:S(2)}) collective-permute-start(bf16[256,256]{0,1:T(8,128)(2,1)S(1)} %pad_maximum_fusion.2), channel_id=1, source_target_pairs={{0,4},{4,8},{8,12},{12,16},{16,20},{20,24},{24,28},{1,5},{5,9},{9,... | collective-permute-start | bytes 393224 | tf_op jit(solution)/shard_map/ppermute | solution.py:33
  71.1 12.0 %collective-permute-start.10 = (bf16[256,256]{0,1:T(8,128)(2,1)S(1)}, bf16[256,256]{0,1:T(8,128)(2,1)S(1)}, u32[]{:S(2)}, u32[]{:S(2)}) collective-permute-start(bf16[256,256]{0,1:T(8,128)(2,1)S(1)} %get-tuple-element.11), channel_id=1, source_target_pairs={{8,0},{12,4},{16,8},{20,12},{24,16},{28,20},{9,1},{13,5},{17,9},{2... | collective-permute-start | bytes 393224 | tf_op jit(solution)/shard_map/ppermute | solution.py:33
  72.4 10.7 %collective-permute-start.9 = (bf16[256,256]{0,1:T(8,128)(2,1)S(1)}, bf16[256,256]{0,1:T(8,128)(2,1)S(1)}, u32[]{:S(2)}, u32[]{:S(2)}) collective-permute-start(bf16[256,256]{0,1:T(8,128)(2,1)S(1)} %get-tuple-element.10), channel_id=1, source_target_pairs={{4,0},{8,4},{12,8},{16,12},{20,16},{24,20},{28,24},{5,1},{9,5},{13... | collective-permute-start | bytes 393224 | tf_op jit(solution)/shard_map/ppermute | solution.py:33
  88.2 96.0 %reduce-scatter.3.cloned.1.call-start = ((), (), s32[]{:S(2)}) async-start(), calls=%async_computation.2 | async-start | bytes 1310720 | tf_op jit(solution)/shard_map/reduce_scatter | solution.py:138
  154.3 13.5 %collective-permute-start.11 = (bf16[96,2048]{1,0:T(8,128)(2,1)S(1)}, bf16[96,2048]{1,0:T(8,128)(2,1)S(1)}, u32[]{:S(2)}, u32[]{:S(2)}) collective-permute-start(bf16[96,2048]{1,0:T(8,128)(2,1)S(1)} %convert_element_type.61), channel_id=1, source_target_pairs={{0,1},{1,0},{2,3},{3,2},{4,5},{5,4},{6,7},{7,6},{8,9},{9,8},{10,11... | collective-permute-start | bytes 1179656 | tf_op jit(solution)/shard_map/ppermute | solution.py:37
Sparse Core Ops, SparseCore 0:
  88.4 64.7 reduce-scatter.4
  156.0 28.1 reduce-scatter.2
